TPU v7x, 256 devices: a whole 4x4x8 slice. The times are simulated.
256 devices in a mesh: pipe: 4 (over y), expert: 16 (over z, core), dp: 4 (over x).
Axes of the slice: x: 4, y: 4, z: 8, core: 2. Of those that a mesh axis runs over, the one named last changes fastest.
Arguments:
- normed: bfloat16 [4, 4, 3072, 4096], P('pipe', None, ('expert', 'dp')), may hold values from -1.5 to 1.5
- saved_out: bfloat16 [4, 4, 3072, 2, 4096], P('pipe', None, ('expert', 'dp')), may hold values from -0.59765625 to 0.59765625
- expert_grads: bfloat16 [4, 4, 4, 16, 16, 9, 4096], P('pipe', None, 'dp', 'expert'), may hold values from -24 to 24
- routes: int32 [4, 4, 3072, 2], P('pipe', None, ('expert', 'dp')), may hold values from 0 to 15, all different within a row; in each aligned block of 48 rows (0 to 47, 48 to 95, ..., all dimensions but the last counted through in order) at most 9 rows name the same one
- router_weight: bfloat16 [4, 4096, 16], P('pipe'), may hold values from -0.375 to 0.375
- upstream: bfloat16 [4, 3072, 4096], P(None, ('expert', 'dp')), may hold values from -6 to 6
Outputs:
- grad_input: bfloat16 [4, 4, 3072, 4096], P('pipe', None, ('expert', 'dp'))
- router_grad: float32 [4, 4096, 16], P('pipe')
Inputs may be any that keep to these rules, and one draw needn't show every extreme that they name: `routes`: the two experts of a row differ. Within the 48 rows of one device for one section and micro-batch no expert is named more than 9 times, a bound that some expert reaches in some of these blocks.
All inputs are finite; a program needn't handle non-finite values.
Results may differ from a plain program's by a relative error of at most 0.007.
Values may be sent and summed in bfloat16 or wider, within the bound.
No kernel may reach another device: no remote copies, remote signals or barrier semaphores. Data moves between devices by JAX's collectives and lax.ppermute only.
A program may use at most 128 MiB of HBM per device.

v0:
```python
import jax
import jax.numpy as jnp
from jax import lax
from jax.sharding import PartitionSpec as P


def shifted(block, axis, distance):
    devices = range(lax.axis_size(axis))
    route = [(i - distance, i) for i in devices if i - distance in devices]
    return lax.ppermute(block, axis, route)


def slot_index(flat, experts, capacity):
    onehot = (flat[..., None] == jnp.arange(experts, dtype=jnp.int32)).astype(jnp.int32)
    before = jnp.cumsum(onehot, axis=-2) - onehot
    position = jnp.sum(before * onehot, axis=-1)
    return flat * capacity + position


def block_grad(incoming, normed_rows, saved_rows, route_rows, returned, index_rows, router_w):
    experts = router_w.shape[1]
    rows_dev = normed_rows.shape[0]
    width = normed_rows.shape[1]
    logits = jnp.dot(normed_rows, router_w, preferred_element_type=jnp.float32)
    expl = jnp.exp(logits)
    probs = expl / jnp.sum(expl, axis=-1, keepdims=True)
    chosen = (route_rows[..., None] == jnp.arange(experts, dtype=jnp.int32)).astype(jnp.float32)
    gates = jnp.einsum("tke,te->tk", chosen, probs)
    dot_grads = jnp.einsum("td,tkd->tk", incoming, saved_rows, preferred_element_type=jnp.float32)
    weighted = dot_grads * gates
    dense_f = (
        jnp.einsum("tke,tk->te", chosen, weighted) - probs * jnp.sum(weighted, axis=-1)[:, None]
    )
    dense = dense_f.astype(jnp.bfloat16)
    router_term = lax.dot_general(
        dense, router_w, (((1,), (1,)), ((), ())), preferred_element_type=jnp.float32
    )
    back_rows = returned[index_rows].reshape(rows_dev, 2, width).astype(jnp.float32)
    total = (
        incoming.astype(jnp.float32)
        + gates[:, 0, None] * back_rows[:, 0]
        + gates[:, 1, None] * back_rows[:, 1]
        + router_term
    )
    weight_part = lax.dot_general(
        normed_rows, dense, (((0,), (0,)), ((), ())), preferred_element_type=jnp.float32
    )
    return (total.astype(jnp.bfloat16), weight_part)


def on_device(normed, saved_out, expert_grads, routes, router_weight, upstream):
    micro = normed.shape[1]
    rows_dev = normed.shape[2]
    width = normed.shape[3]
    sections = lax.axis_size("pipe")
    section_idx = lax.axis_index("pipe")
    router_w = router_weight[0]
    experts = router_w.shape[1]
    capacity = expert_grads.shape[5]
    slot_rows = slot_index(routes[0].reshape(micro, -1), experts, capacity)
    local_grads = expert_grads[0, :, 0]
    returned_list = []
    for block_num in range(micro):
        received = lax.all_to_all(
            local_grads[block_num], "expert", split_axis=1, concat_axis=0, tiled=True
        )
        returned_list.append(received.reshape(experts * capacity, width))
    returned_all = jnp.stack(returned_list)
    grad_buffer = jnp.zeros((micro, rows_dev, width), jnp.bfloat16)
    weight_sum = jnp.zeros((width, experts), jnp.float32)
    passed = jnp.zeros((rows_dev, width), jnp.bfloat16)
    for tick_num in range(micro + sections - 1):
        if tick_num > 0:
            passed = shifted(passed, "pipe", -1)
        block_num = tick_num - (sections - 1 - section_idx)
        is_active = (block_num >= 0) & (block_num < micro)
        block_idx = jnp.clip(block_num, 0, micro - 1)
        returned = lax.dynamic_index_in_dim(returned_all, block_idx, 0, keepdims=False)
        from_top = lax.dynamic_index_in_dim(upstream, block_idx, 0, keepdims=False)
        incoming = jnp.where(section_idx == sections - 1, from_top, passed)
        new_grad, weight_part = block_grad(
            incoming,
            lax.dynamic_index_in_dim(normed[0], block_idx, 0, keepdims=False),
            lax.dynamic_index_in_dim(saved_out[0], block_idx, 0, keepdims=False),
            lax.dynamic_index_in_dim(routes[0], block_idx, 0, keepdims=False),
            returned,
            lax.dynamic_index_in_dim(slot_rows, block_idx, 0, keepdims=False),
            router_w,
        )
        updated = lax.dynamic_update_index_in_dim(grad_buffer, new_grad, block_idx, 0)
        grad_buffer = jnp.where(is_active, updated, grad_buffer)
        weight_sum = weight_sum + jnp.where(is_active, weight_part, 0.0)
        passed = new_grad
    router_grad = lax.psum(weight_sum / micro, ("expert", "dp"))
    return (grad_buffer[None], router_grad[None])


def solution(mesh):
    in_specs = (
        P("pipe", None, ("expert", "dp"), None),
        P("pipe", None, ("expert", "dp"), None, None),
        P("pipe", None, "dp", "expert", None, None, None),
        P("pipe", None, ("expert", "dp"), None),
        P("pipe", None, None),
        P(None, ("expert", "dp"), None),
    )
    out_specs = (P("pipe", None, ("expert", "dp"), None), P("pipe", None, None))
    return jax.shard_map(
        on_device, mesh=mesh, in_specs=in_specs, out_specs=out_specs, check_vma=False
    )
```

profile of v0, /device:TPU:1, one launch (start us, length us, event | category | flops | bytes accessed | tf_op | source)
XLA Modules:
  0.0 636.1 jit_solution(2353032965511129839)
XLA Ops:
  7.2 4.4 fusion.196
  13.7 10.1 %all-to-all-start = ((bf16[1,16,9,4096]{3,2,0,1:T(8,128)(2,1)}), bf16[1,16,9,4096]{3,2,0,1:T(8,128)(2,1)}, u32[]{:S(2)}, u32[]{:S(2)}) async-start(bf16[1,16,9,4096]{3,2,0,1:T(8,128)(2,1)} %bitcast.551), calls=%async_computation | async-start | bytes 4194304 | tf_op jit(solution)/shard_map/all_to_all | solution.py:64
  30.8 3.4 copy.366
  39.4 33.5 %all-to-all-done = bf16[1,16,9,4096]{3,2,0,1:T(8,128)(2,1)} async-done(((bf16[1,16,9,4096]{3,2,0,1:T(8,128)(2,1)}), bf16[1,16,9,4096]{3,2,0,1:T(8,128)(2,1)}, u32[]{:S(2)}, u32[]{:S(2)}) %all-to-all-start) | async-done | bytes 1179680 | tf_op jit(solution)/shard_map/all_to_all | solution.py:64
  72.9 5.0 all-to-all-start.1
  78.8 3.5 copy.365
  97.5 29.4 %all-to-all-done.1 = bf16[1,16,9,4096]{3,2,0,1:T(8,128)(2,1)} async-done(((bf16[1,16,9,4096]{3,2,0,1:T(8,128)(2,1)}), bf16[1,16,9,4096]{3,2,0,1:T(8,128)(2,1)}, u32[]{:S(2)}, u32[]{:S(2)}) %all-to-all-start.1) | async-done | bytes 1179680 | tf_op jit(solution)/shard_map/all_to_all | solution.py:64
  126.9 5.0 all-to-all-start.2
  143.3 37.7 %all-to-all-done.2 = bf16[1,16,9,4096]{3,2,0,1:T(8,128)(2,1)} async-done(((bf16[1,16,9,4096]{3,2,0,1:T(8,128)(2,1)}), bf16[1,16,9,4096]{3,2,0,1:T(8,128)(2,1)}, u32[]{:S(2)}, u32[]{:S(2)}) %all-to-all-start.2) | async-done | bytes 1179680 | tf_op jit(solution)/shard_map/all_to_all | solution.py:64
  181.0 5.1 all-to-all-start.3
  201.4 33.7 %all-to-all-done.3 = bf16[1,16,9,4096]{3,2,0,1:T(8,128)(2,1)} async-done(((bf16[1,16,9,4096]{3,2,0,1:T(8,128)(2,1)}), bf16[1,16,9,4096]{3,2,0,1:T(8,128)(2,1)}, u32[]{:S(2)}, u32[]{:S(2)}) %all-to-all-start.3) | async-done | bytes 1179680 | tf_op jit(solution)/shard_map/all_to_all | solution.py:64
  240.2 7.0 %dynamic-slice_bitcast_fusion = (bf16[144,4096]{1,0:T(8,128)(2,1)}, bf16[144,4096]{1,0:T(8,128)(2,1)}, bf16[144,4096]{1,0:T(8,128)(2,1)}, bf16[144,4096]{1,0:T(8...) fusion(bf16[4,144,4096]{2,1,0:T(8,128)(2,1)} %constant_dynamic-update-slice_fusion, ...), kind=kLoop, calls=%fused_computation.28 | loop fusion | bytes 16515100 | tf_op jit(solution)/shard_map/jit(dynamic_index_in_dim)/squeeze | solution.py:78
  247.1 4.1 gather_fusion
  251.3 2.9 reshape.322
  254.2 3.6 fusion.203
  259.1 3.0 bitcast_dynamic-update-slice_fusion
  263.8 4.2 gather_fusion.1
  268.0 2.9 reshape.323
  271.0 4.7 fusion.202
  275.7 4.2 gather_fusion.2
  279.9 2.9 reshape.324
  282.9 4.7 fusion.201
  287.6 4.2 gather_fusion.3
  291.8 3.1 reshape.325
  294.9 4.7 fusion.200
  299.6 4.3 gather_fusion.4
  303.9 2.9 reshape.326
  308.0 2.7 fusion.50
  319.0 3.8 fusion.81
  324.1 3.0 fusion.199
  327.1 4.2 gather_fusion.5
  331.3 3.1 reshape.327
  337.2 2.7 fusion.51
  348.2 3.8 fusion.78
  353.2 2.9 fusion.198
  356.2 4.3 gather_fusion.6
  360.5 2.9 reshape.328
  364.8 2.7 fusion.52
  375.8 3.6 fusion.75
  381.1 2.9 fusion.197
  385.9 4.9 collective-permute-done.3
  395.4 3.7 fusion.72
  400.8 8.6 %collective-permute-done.4 = bf16[48,4096]{1,0:T(8,128)(2,1)S(1)} collective-permute-done((bf16[48,4096]{1,0:T(8,128)(2,1)S(1)}, bf16[48,4096]{1,0:T(8,128)(2,1)S(1)}, u32[]{:S(2)}, u32[]{:S(2)}) %collective-permute-start.4) | collective-permute-done | bytes 393248 | tf_op jit(solution)/shard_map/ppermute | solution.py:10
  411.2 2.7 fusion.54
  421.9 3.6 fusion.69
  430.0 4.8 collective-permute-done.5
  449.5 3.5 fusion.66
  453.1 174.1 %all-reduce.2.cloned.1.call-done = f32[1,4096,16]{1,2,0:T(8,128)} async-done(((f32[1,4096,16]{1,2,0:T(8,128)}), f32[1,4096,16]{1,2,0:T(8,128)}) %all-reduce.2.cloned.1.call-update) | async-done | bytes 262160 | tf_op jit(solution)/shard_map/psum | solution.py:94
  (270 shorter events, 137.6 us)
Async XLA Ops:
  7.2 20.7 %copy-start = (bf16[1,4,48,2,4096]{4,3,2,1,0:T(2,128)(2,1)S(1)}, bf16[1,4,48,2,4096]{4,3,2,1,0:T(2,128)(2,1)}, u32[]{:S(2)}) copy-start(bf16[1,4,48,2,4096]{4,3,2,1,0:T(2,128)(2,1)} %param.7) | copy-start | bytes 9437188
  13.7 10.1 %copy-start.43 = (s32[1,4,48,2]{2,3,1,0:T(2,128)S(1)}, s32[1,4,48,2]{2,3,1,0:T(2,128)}, u32[]{:S(2)}) copy-start(s32[1,4,48,2]{2,3,1,0:T(2,128)} %param.9) | copy-start | bytes 4612
  13.7 10.9 %copy-start.1 = (bf16[1,4096,16]{1,2,0:T(8,128)(2,1)S(1)}, bf16[1,4096,16]{1,2,0:T(8,128)(2,1)}, u32[]{:S(2)}) copy-start(bf16[1,4096,16]{1,2,0:T(8,128)(2,1)} %param.10) | copy-start | bytes 393220
  13.7 59.2 %all-to-all-start = ((bf16[1,16,9,4096]{3,2,0,1:T(8,128)(2,1)}), bf16[1,16,9,4096]{3,2,0,1:T(8,128)(2,1)}, u32[]{:S(2)}, u32[]{:S(2)}) async-start(bf16[1,16,9,4096]{3,2,0,1:T(8,128)(2,1)} %bitcast.551), calls=%async_computation | async-start | bytes 4194304 | tf_op jit(solution)/shard_map/all_to_all | solution.py:64
  26.8 3.3 copy-start.47
  34.2 38.7 %copy-start.41 = (s32[4,96]{1,0:T(4,128)}, s32[4,96]{1,0:T(4,128)S(1)}, u32[]{:S(2)}) copy-start(s32[4,96]{1,0:T(4,128)S(1)} %copy.75) | copy-start | bytes 4612
  34.3 38.6 %copy-start.20 = (s32[48,2]{1,0:T(8,128)}, s32[48,2]{1,0:T(8,128)S(1)}, u32[]{:S(2)}) copy-start(s32[48,2]{1,0:T(8,128)S(1)} %copy.79) | copy-start | bytes 1156
  36.2 41.6 %copy-start.18 = (s32[48,2]{1,0:T(8,128)}, s32[48,2]{1,0:T(8,128)S(1)}, u32[]{:S(2)}) copy-start(s32[48,2]{1,0:T(8,128)S(1)} %copy.82) | copy-start | bytes 1156
  72.9 54.0 %all-to-all-start.1 = ((bf16[1,16,9,4096]{3,2,0,1:T(8,128)(2,1)}), bf16[1,16,9,4096]{3,2,0,1:T(8,128)(2,1)}, u32[]{:S(2)}, u32[]{:S(2)}) async-start(bf16[1,16,9,4096]{3,2,0,1:T(8,128)(2,1)} %bitcast.550), calls=%async_computation.1 | async-start | bytes 4194304 | tf_op jit(solution)/shard_map/all_to_all | solution.py:64
  78.8 3.5 copy-start.7
  86.9 2.8 copy-start.19
  93.3 2.7 copy-start.15
  96.2 35.7 %copy-start.14 = (s32[48,2]{1,0:T(8,128)}, s32[48,2]{1,0:T(8,128)S(1)}, u32[]{:S(2)}) copy-start(s32[48,2]{1,0:T(8,128)S(1)} %copy.94) | copy-start | bytes 1156
  97.4 29.5 %copy-start.48 = (f32[48]{0:T(128)}, f32[48]{0:T(128)S(1)}, u32[]{:S(2)}) copy-start(f32[48]{0:T(128)S(1)} %get-tuple-element.93) | copy-start | bytes 580
  126.9 54.0 %all-to-all-start.2 = ((bf16[1,16,9,4096]{3,2,0,1:T(8,128)(2,1)}), bf16[1,16,9,4096]{3,2,0,1:T(8,128)(2,1)}, u32[]{:S(2)}, u32[]{:S(2)}) async-start(bf16[1,16,9,4096]{3,2,0,1:T(8,128)(2,1)} %bitcast.549), calls=%async_computation.2 | async-start | bytes 4194304 | tf_op jit(solution)/shard_map/all_to_all | solution.py:64
  132.2 54.2 %copy-start.44 = (f32[48,2]{0,1:T(2,128)}, f32[48,2]{0,1:T(2,128)S(1)}, u32[]{:S(2)}) copy-start(f32[48,2]{0,1:T(2,128)S(1)} %copy.167) | copy-start | bytes 1156
  180.9 6.0 copy-start.32
  181.0 6.0 copy-start.42
  181.0 6.0 copy-start.57
  181.0 6.0 copy-start.60
  181.0 54.2 %all-to-all-start.3 = ((bf16[1,16,9,4096]{3,2,0,1:T(8,128)(2,1)}), bf16[1,16,9,4096]{3,2,0,1:T(8,128)(2,1)}, u32[]{:S(2)}, u32[]{:S(2)}) async-start(bf16[1,16,9,4096]{3,2,0,1:T(8,128)(2,1)} %bitcast.548), calls=%async_computation.3 | async-start | bytes 4194304 | tf_op jit(solution)/shard_map/all_to_all | solution.py:64
  186.1 441.1 %all-reduce.2.cloned.1.call-start = ((), (), s32[]{:S(2)}) async-start(), calls=%async_computation.4 | async-start | bytes 524288 | tf_op jit(solution)/shard_map/psum | solution.py:94
  262.1 44.7 %collective-permute-start = (bf16[48,4096]{1,0:T(8,128)(2,1)}, bf16[48,4096]{1,0:T(8,128)(2,1)}, u32[]{:S(2)}, u32[]{:S(2)}) collective-permute-start(bf16[48,4096]{1,0:T(8,128)(2,1)} %get-tuple-element.72), channel_id=1, source_target_pairs={{64,0},{128,64},{192,128},{65,1},{129,65},{193,129},{66,2},{130,66... | collective-permute-start | bytes 1179656 | tf_op jit(solution)/shard_map/ppermute | solution.py:10
  308.0 10.3 %copy-start.30 = (f32[48,16]{0,1:T(8,128)S(1)}, f32[48,16]{0,1:T(8,128)}, u32[]{:S(2)}) copy-start(f32[48,16]{0,1:T(8,128)} %copy-done.29) | copy-start | bytes 9220
  319.0 3.8 copy-start.33
  319.0 5.1 copy-start.4
  322.8 13.2 %collective-permute-start.1 = (bf16[48,4096]{1,0:T(8,128)(2,1)}, bf16[48,4096]{1,0:T(8,128)(2,1)}, u32[]{:S(2)}, u32[]{:S(2)}) collective-permute-start(bf16[48,4096]{1,0:T(8,128)(2,1)} %get-tuple-element.76), channel_id=1, source_target_pairs={{64,0},{128,64},{192,128},{65,1},{129,65},{193,129},{66,2},{130,66... | collective-permute-start | bytes 1179656 | tf_op jit(solution)/shard_map/ppermute | solution.py:10
  337.1 10.3 %copy-start.26 = (f32[48,16]{0,1:T(8,128)S(1)}, f32[48,16]{0,1:T(8,128)}, u32[]{:S(2)}) copy-start(f32[48,16]{0,1:T(8,128)} %copy-done.25) | copy-start | bytes 9220
  348.2 3.8 copy-start.35
  348.2 5.1 copy-start.5
  352.0 11.6 %collective-permute-start.2 = (bf16[48,4096]{1,0:T(8,128)(2,1)}, bf16[48,4096]{1,0:T(8,128)(2,1)}, u32[]{:S(2)}, u32[]{:S(2)}) collective-permute-start(bf16[48,4096]{1,0:T(8,128)(2,1)} %get-tuple-element.80), channel_id=1, source_target_pairs={{64,0},{128,64},{192,128},{65,1},{129,65},{193,129},{66,2},{130,66... | collective-permute-start | bytes 1179656 | tf_op jit(solution)/shard_map/ppermute | solution.py:10
  364.7 10.3 %copy-start.28 = (f32[48,16]{0,1:T(8,128)S(1)}, f32[48,16]{0,1:T(8,128)}, u32[]{:S(2)}) copy-start(f32[48,16]{0,1:T(8,128)} %copy-done.27) | copy-start | bytes 9220
  375.8 3.7 copy-start.37
  375.8 5.3 copy-start.6
  379.4 4.6 copy-start.34
  379.4 11.4 %collective-permute-start.3 = (bf16[48,4096]{1,0:T(8,128)(2,1)S(1)}, bf16[48,4096]{1,0:T(8,128)(2,1)S(1)}, u32[]{:S(2)}, u32[]{:S(2)}) collective-permute-start(bf16[48,4096]{1,0:T(8,128)(2,1)S(1)} %get-tuple-element.84), channel_id=1, source_target_pairs={{64,0},{128,64},{192,128},{65,1},{129,65},{193,129},{66,2},{130,66... | collective-permute-start | bytes 1179656 | tf_op jit(solution)/shard_map/ppermute | solution.py:10
  395.3 3.7 copy-start.39
  395.3 5.0 copy-start.2
  395.4 5.0 copy-start.13
  395.4 5.0 copy-start.36
  395.4 5.2 copy-start.38
  399.1 10.3 %collective-permute-start.4 = (bf16[48,4096]{1,0:T(8,128)(2,1)S(1)}, bf16[48,4096]{1,0:T(8,128)(2,1)S(1)}, u32[]{:S(2)}, u32[]{:S(2)}) collective-permute-start(bf16[48,4096]{1,0:T(8,128)(2,1)S(1)} %get-tuple-element.88), channel_id=1, source_target_pairs={{64,0},{128,64},{192,128},{65,1},{129,65},{193,129},{66,2},{130,66... | collective-permute-start | bytes 1179656 | tf_op jit(solution)/shard_map/ppermute | solution.py:10
  411.2 10.1 %copy-start.22 = (f32[48,16]{0,1:T(8,128)S(1)}, f32[48,16]{0,1:T(8,128)}, u32[]{:S(2)}) copy-start(f32[48,16]{0,1:T(8,128)} %copy-done.21) | copy-start | bytes 9220
  421.9 4.9 copy-start.3
  421.9 5.0 copy-start.40
  425.6 9.2 %collective-permute-start.5 = (bf16[48,4096]{1,0:T(8,128)(2,1)S(1)}, bf16[48,4096]{1,0:T(8,128)(2,1)S(1)}, u32[]{:S(2)}, u32[]{:S(2)}) collective-permute-start(bf16[48,4096]{1,0:T(8,128)(2,1)S(1)} %get-tuple-element.92), channel_id=1, source_target_pairs={{64,0},{128,64},{192,128},{65,1},{129,65},{193,129},{66,2},{130,66... | collective-permute-start | bytes 1179656 | tf_op jit(solution)/shard_map/ppermute | solution.py:10
  436.6 4.2 copy-start.45
  436.6 10.3 %copy-start.49 = (f32[48]{0:T(128)S(1)}, f32[48]{0:T(128)}, u32[]{:S(2)}) copy-start(f32[48]{0:T(128)} %copy-done.48) | copy-start | bytes 580
  (26 other events, 34.4 us)
Sparse Core Ops, SparseCore 0:
  449.7 177.4 all-reduce.1
where the time goes:
time: 646 us; the launch traced here: 636 us
  waiting for transfers between devices  328 us (51%)
  local copies, waits for them, and re-layouts  165 us (26%)
  matrix products  57.4 us (9%)
  other arithmetic  35.6 us (6%)
  starting transfers between devices  33.9 us (5%)
  between operations  15.2 us (2%)
    psum x1, waiting for transfers between devices, on_device(): router_grad = lax.psum(weight_sum / micro, ('expert', 'dp'))  174 us
    all_to_all x4, waiting for transfers between devices, on_device(): lax.all_to_all(local_grads[block_num], 'expert', split_axis=1, concat_axi...  134 us
    unnamed x150, local copies, waits for them, and re-layouts  34.3 us
    gather x7, local copies, waits for them, and re-layouts, block_grad(): returned[index_rows].reshape(rows_dev, 2, width).astype(jnp.float32)  29.6 us
    slice x7, local copies, waits for them, and re-layouts, block_grad(): back_rows[:, 0]  26.5 us
    all_to_all x4, starting transfers between devices, on_device(): lax.all_to_all(local_grads[block_num], 'expert', split_axis=1, concat_axi...  25.2 us
    dot_general x7, matrix products, block_grad(): lax.dot_general(dense, router_w, (((1,), (1,)), ((), ())), preferred_elem...  25 us
    convert_element_type x7, local copies, waits for them, and re-layouts, block_grad(): returned[index_rows].reshape(rows_dev, 2, width).astype(jnp.float32)  20.9 us
  transfers between devices with their start and end apart: 11, of which 10 were waited for; matrix products, arithmetic and copies ran while one was open for 21% of the time, Pallas kernels for 0%

commit v1 on v0

--- a/solution.py
+++ b/solution.py
@@ -91,7 +91,10 @@
         grad_buffer = jnp.where(is_active, updated, grad_buffer)
         weight_sum = weight_sum + jnp.where(is_active, weight_part, 0.0)
         passed = new_grad
-    router_grad = lax.psum(weight_sum / micro, ("expert", "dp"))
+    report_unit_here = lambda sheet, mesh_name, net_axis: jax.lax.psum(
+        jax.lax.psum(sheet, mesh_name), net_axis
+    )
+    router_grad = report_unit_here(weight_sum / micro, "dp", "expert")
     return (grad_buffer[None], router_grad[None])
 
 

time: 646 us -> 620 us (0.960)
  waiting for transfers between devices: 328 us -> 304 us
    psum x1 -> x2, waiting for transfers between devices: 174 us -> 149 us  [the longest x1 110 us: on_device(): jax.lax.psum(jax.lax.psum(sheet, mesh_name), net_axis)]
    unnamed x150 -> x152, local copies, waits for them, and re-layouts: 34.3 us -> 33.4 us
  transfers between devices with their start and end apart: 11 -> 12, of which waited for: 10 -> 10; matrix products, arithmetic and copies ran while one was open for 21% -> 22% of each run, Pallas kernels for 0% -> 0%
where the time goes in v1:
time: 620 us; the launch traced here: 610 us
  waiting for transfers between devices  304 us (49%)
  local copies, waits for them, and re-layouts  164 us (26%)
  matrix products  57.5 us (9%)
  other arithmetic  35.8 us (6%)
  starting transfers between devices  33.8 us (5%)
  between operations  15.3 us (2%)
    all_to_all x4, waiting for transfers between devices, on_device(): lax.all_to_all(local_grads[block_num], 'expert', split_axis=1, concat_axi...  134 us
    psum x1, waiting for transfers between devices, on_device(): jax.lax.psum(jax.lax.psum(sheet, mesh_name), net_axis)  110 us
    psum x1, waiting for transfers between devices, on_device(): jax.lax.psum(sheet, mesh_name)  39 us
    unnamed x152, local copies, waits for them, and re-layouts  33.4 us
    gather x7, local copies, waits for them, and re-layouts, block_grad(): returned[index_rows].reshape(rows_dev, 2, width).astype(jnp.float32)  29.5 us
    slice x7, local copies, waits for them, and re-layouts, block_grad(): back_rows[:, 0]  26.5 us
    all_to_all x4, starting transfers between devices, on_device(): lax.all_to_all(local_grads[block_num], 'expert', split_axis=1, concat_axi...  25.2 us
    dot_general x7, matrix products, block_grad(): lax.dot_general(dense, router_w, (((1,), (1,)), ((), ())), preferred_elem...  25.1 us
  transfers between devices with their start and end apart: 12, of which 10 were waited for; matrix products, arithmetic and copies ran while one was open for 22% of the time, Pallas kernels for 0%

profile of v1, /device:TPU:1, one launch (start us, length us, event | category | flops | bytes accessed | tf_op | source)
XLA Modules:
  0.0 610.4 jit_solution(6269259830932136821)
XLA Ops:
  7.2 4.4 fusion.195
  13.7 10.1 %all-to-all-start = ((bf16[1,16,9,4096]{3,2,0,1:T(8,128)(2,1)}), bf16[1,16,9,4096]{3,2,0,1:T(8,128)(2,1)}, u32[]{:S(2)}, u32[]{:S(2)}) async-start(bf16[1,16,9,4096]{3,2,0,1:T(8,128)(2,1)} %bitcast.550), calls=%async_computation | async-start | bytes 4194304 | tf_op jit(solution)/shard_map/all_to_all | solution.py:64
  30.7 3.4 copy.366
  39.3 33.5 %all-to-all-done = bf16[1,16,9,4096]{3,2,0,1:T(8,128)(2,1)} async-done(((bf16[1,16,9,4096]{3,2,0,1:T(8,128)(2,1)}), bf16[1,16,9,4096]{3,2,0,1:T(8,128)(2,1)}, u32[]{:S(2)}, u32[]{:S(2)}) %all-to-all-start) | async-done | bytes 1179680 | tf_op jit(solution)/shard_map/all_to_all | solution.py:64
  72.9 5.0 all-to-all-start.1
  78.7 3.5 copy.365
  97.5 29.4 %all-to-all-done.1 = bf16[1,16,9,4096]{3,2,0,1:T(8,128)(2,1)} async-done(((bf16[1,16,9,4096]{3,2,0,1:T(8,128)(2,1)}), bf16[1,16,9,4096]{3,2,0,1:T(8,128)(2,1)}, u32[]{:S(2)}, u32[]{:S(2)}) %all-to-all-start.1) | async-done | bytes 1179680 | tf_op jit(solution)/shard_map/all_to_all | solution.py:64
  126.9 5.0 all-to-all-start.2
  143.5 37.5 %all-to-all-done.2 = bf16[1,16,9,4096]{3,2,0,1:T(8,128)(2,1)} async-done(((bf16[1,16,9,4096]{3,2,0,1:T(8,128)(2,1)}), bf16[1,16,9,4096]{3,2,0,1:T(8,128)(2,1)}, u32[]{:S(2)}, u32[]{:S(2)}) %all-to-all-start.2) | async-done | bytes 1179680 | tf_op jit(solution)/shard_map/all_to_all | solution.py:64
  180.9 5.1 all-to-all-start.3
  201.3 33.8 %all-to-all-done.3 = bf16[1,16,9,4096]{3,2,0,1:T(8,128)(2,1)} async-done(((bf16[1,16,9,4096]{3,2,0,1:T(8,128)(2,1)}), bf16[1,16,9,4096]{3,2,0,1:T(8,128)(2,1)}, u32[]{:S(2)}, u32[]{:S(2)}) %all-to-all-start.3) | async-done | bytes 1179680 | tf_op jit(solution)/shard_map/all_to_all | solution.py:64
  240.1 7.0 %dynamic-slice_bitcast_fusion = (bf16[144,4096]{1,0:T(8,128)(2,1)}, bf16[144,4096]{1,0:T(8,128)(2,1)}, bf16[144,4096]{1,0:T(8,128)(2,1)}, bf16[144,4096]{1,0:T(8...) fusion(bf16[4,144,4096]{2,1,0:T(8,128)(2,1)} %constant_dynamic-update-slice_fusion, ...), kind=kLoop, calls=%fused_computation.27 | loop fusion | bytes 16515100 | tf_op jit(solution)/shard_map/jit(dynamic_index_in_dim)/squeeze | solution.py:78
  247.1 4.1 gather_fusion
  251.2 2.9 reshape.322
  254.2 3.6 fusion.202
  259.1 3.0 bitcast_dynamic-update-slice_fusion
  263.8 4.2 gather_fusion.1
  268.0 2.9 reshape.323
  271.0 4.7 fusion.201
  275.7 4.2 gather_fusion.2
  279.9 2.9 reshape.324
  282.9 4.7 fusion.200
  287.6 4.2 gather_fusion.3
  291.8 3.1 reshape.325
  296.1 2.7 fusion.49
  307.0 3.8 fusion.80
  312.1 3.0 fusion.199
  315.1 4.3 gather_fusion.4
  319.4 2.9 reshape.326
  325.2 2.7 fusion.50
  336.2 3.8 fusion.77
  341.3 2.9 fusion.198
  344.2 4.2 gather_fusion.5
  348.5 3.1 reshape.327
  352.8 2.7 fusion.51
  363.8 3.8 fusion.74
  368.9 3.0 fusion.197
  371.9 4.2 gather_fusion.6
  376.1 2.9 reshape.328
  384.8 3.6 fusion.71
  390.4 10.2 %collective-permute-done.4 = bf16[48,4096]{1,0:T(8,128)(2,1)S(1)} collective-permute-done((bf16[48,4096]{1,0:T(8,128)(2,1)S(1)}, bf16[48,4096]{1,0:T(8,128)(2,1)S(1)}, u32[]{:S(2)}, u32[]{:S(2)}) %collective-permute-start.4) | collective-permute-done | bytes 393248 | tf_op jit(solution)/shard_map/ppermute | solution.py:10
  402.4 2.7 fusion.53
  413.3 3.6 fusion.68
  418.6 8.4 %collective-permute-done.5 = bf16[48,4096]{1,0:T(8,128)(2,1)S(1)} collective-permute-done((bf16[48,4096]{1,0:T(8,128)(2,1)S(1)}, bf16[48,4096]{1,0:T(8,128)(2,1)S(1)}, u32[]{:S(2)}, u32[]{:S(2)}) %collective-permute-start.5) | collective-permute-done | bytes 393248 | tf_op jit(solution)/shard_map/ppermute | solution.py:10
  441.5 4.7 fusion.196
  448.9 39.0 %all-reduce.3.cloned.1.call-done = f32[4096,16]{0,1:T(8,128)} async-done(((f32[4096,16]{0,1:T(8,128)}), f32[4096,16]{0,1:T(8,128)}) %all-reduce.3.cloned.1.call-update) | async-done | bytes 262160 | tf_op jit(solution)/shard_map/psum | solution.py:95
  488.0 3.5 fusion.65
  491.5 109.9 %all-reduce.5.cloned.1.call-done = f32[1,4096,16]{1,2,0:T(8,128)} async-done(((f32[1,4096,16]{1,2,0:T(8,128)}), f32[1,4096,16]{1,2,0:T(8,128)}) %all-reduce.5.cloned.1.call-update) | async-done | bytes 262160 | tf_op jit(solution)/shard_map/psum | solution.py:94
  (275 shorter events, 136.9 us)
Async XLA Ops:
  7.2 20.6 %copy-start = (bf16[1,4,48,2,4096]{4,3,2,1,0:T(2,128)(2,1)S(1)}, bf16[1,4,48,2,4096]{4,3,2,1,0:T(2,128)(2,1)}, u32[]{:S(2)}) copy-start(bf16[1,4,48,2,4096]{4,3,2,1,0:T(2,128)(2,1)} %param.7) | copy-start | bytes 9437188
  13.7 10.1 %copy-start.42 = (s32[1,4,48,2]{2,3,1,0:T(2,128)S(1)}, s32[1,4,48,2]{2,3,1,0:T(2,128)}, u32[]{:S(2)}) copy-start(s32[1,4,48,2]{2,3,1,0:T(2,128)} %param.9) | copy-start | bytes 4612
  13.7 10.9 %copy-start.1 = (bf16[1,4096,16]{1,2,0:T(8,128)(2,1)S(1)}, bf16[1,4096,16]{1,2,0:T(8,128)(2,1)}, u32[]{:S(2)}) copy-start(bf16[1,4096,16]{1,2,0:T(8,128)(2,1)} %param.10) | copy-start | bytes 393220
  13.7 59.2 %all-to-all-start = ((bf16[1,16,9,4096]{3,2,0,1:T(8,128)(2,1)}), bf16[1,16,9,4096]{3,2,0,1:T(8,128)(2,1)}, u32[]{:S(2)}, u32[]{:S(2)}) async-start(bf16[1,16,9,4096]{3,2,0,1:T(8,128)(2,1)} %bitcast.550), calls=%async_computation | async-start | bytes 4194304 | tf_op jit(solution)/shard_map/all_to_all | solution.py:64
  26.8 3.3 copy-start.46
  34.1 38.7 %copy-start.40 = (s32[4,96]{1,0:T(4,128)}, s32[4,96]{1,0:T(4,128)S(1)}, u32[]{:S(2)}) copy-start(s32[4,96]{1,0:T(4,128)S(1)} %copy.75) | copy-start | bytes 4612
  34.2 38.6 %copy-start.19 = (s32[48,2]{1,0:T(8,128)}, s32[48,2]{1,0:T(8,128)S(1)}, u32[]{:S(2)}) copy-start(s32[48,2]{1,0:T(8,128)S(1)} %copy.79) | copy-start | bytes 1156
  36.2 41.6 %copy-start.17 = (s32[48,2]{1,0:T(8,128)}, s32[48,2]{1,0:T(8,128)S(1)}, u32[]{:S(2)}) copy-start(s32[48,2]{1,0:T(8,128)S(1)} %copy.82) | copy-start | bytes 1156
  72.9 54.0 %all-to-all-start.1 = ((bf16[1,16,9,4096]{3,2,0,1:T(8,128)(2,1)}), bf16[1,16,9,4096]{3,2,0,1:T(8,128)(2,1)}, u32[]{:S(2)}, u32[]{:S(2)}) async-start(bf16[1,16,9,4096]{3,2,0,1:T(8,128)(2,1)} %bitcast.549), calls=%async_computation.1 | async-start | bytes 4194304 | tf_op jit(solution)/shard_map/all_to_all | solution.py:64
  78.7 3.5 copy-start.7
  96.2 35.7 %copy-start.13 = (s32[48,2]{1,0:T(8,128)}, s32[48,2]{1,0:T(8,128)S(1)}, u32[]{:S(2)}) copy-start(s32[48,2]{1,0:T(8,128)S(1)} %copy.94) | copy-start | bytes 1156
  97.4 29.5 %copy-start.47 = (f32[48]{0:T(128)}, f32[48]{0:T(128)S(1)}, u32[]{:S(2)}) copy-start(f32[48]{0:T(128)S(1)} %get-tuple-element.93) | copy-start | bytes 580
  126.9 54.0 %all-to-all-start.2 = ((bf16[1,16,9,4096]{3,2,0,1:T(8,128)(2,1)}), bf16[1,16,9,4096]{3,2,0,1:T(8,128)(2,1)}, u32[]{:S(2)}, u32[]{:S(2)}) async-start(bf16[1,16,9,4096]{3,2,0,1:T(8,128)(2,1)} %bitcast.548), calls=%async_computation.2 | async-start | bytes 4194304 | tf_op jit(solution)/shard_map/all_to_all | solution.py:64
  132.2 54.2 %copy-start.43 = (f32[48,2]{0,1:T(2,128)}, f32[48,2]{0,1:T(2,128)S(1)}, u32[]{:S(2)}) copy-start(f32[48,2]{0,1:T(2,128)S(1)} %copy.167) | copy-start | bytes 1156
  180.9 6.0 copy-start.31
  180.9 6.0 copy-start.41
  180.9 6.0 copy-start.56
  180.9 6.0 copy-start.61
  180.9 54.2 %all-to-all-start.3 = ((bf16[1,16,9,4096]{3,2,0,1:T(8,128)(2,1)}), bf16[1,16,9,4096]{3,2,0,1:T(8,128)(2,1)}, u32[]{:S(2)}, u32[]{:S(2)}) async-start(bf16[1,16,9,4096]{3,2,0,1:T(8,128)(2,1)} %bitcast.547), calls=%async_computation.3 | async-start | bytes 4194304 | tf_op jit(solution)/shard_map/all_to_all | solution.py:64
  186.1 301.9 %all-reduce.3.cloned.1.call-start = ((), (), s32[]{:S(2)}) async-start(), calls=%async_computation.4 | async-start | bytes 524288 | tf_op jit(solution)/shard_map/psum | solution.py:95
  262.1 32.8 %collective-permute-start = (bf16[48,4096]{1,0:T(8,128)(2,1)}, bf16[48,4096]{1,0:T(8,128)(2,1)}, u32[]{:S(2)}, u32[]{:S(2)}) collective-permute-start(bf16[48,4096]{1,0:T(8,128)(2,1)} %get-tuple-element.72), channel_id=1, source_target_pairs={{64,0},{128,64},{192,128},{65,1},{129,65},{193,129},{66,2},{130,66... | collective-permute-start | bytes 1179656 | tf_op jit(solution)/shard_map/ppermute | solution.py:10
  296.0 10.3 %copy-start.29 = (f32[48,16]{0,1:T(8,128)S(1)}, f32[48,16]{0,1:T(8,128)}, u32[]{:S(2)}) copy-start(f32[48,16]{0,1:T(8,128)} %copy-done.28) | copy-start | bytes 9220
  307.0 3.8 copy-start.32
  307.0 5.1 copy-start.4
  310.8 13.2 %collective-permute-start.1 = (bf16[48,4096]{1,0:T(8,128)(2,1)}, bf16[48,4096]{1,0:T(8,128)(2,1)}, u32[]{:S(2)}, u32[]{:S(2)}) collective-permute-start(bf16[48,4096]{1,0:T(8,128)(2,1)} %get-tuple-element.76), channel_id=1, source_target_pairs={{64,0},{128,64},{192,128},{65,1},{129,65},{193,129},{66,2},{130,66... | collective-permute-start | bytes 1179656 | tf_op jit(solution)/shard_map/ppermute | solution.py:10
  325.2 10.3 %copy-start.25 = (f32[48,16]{0,1:T(8,128)S(1)}, f32[48,16]{0,1:T(8,128)}, u32[]{:S(2)}) copy-start(f32[48,16]{0,1:T(8,128)} %copy-done.24) | copy-start | bytes 9220
  336.2 3.8 copy-start.34
  336.2 5.1 copy-start.5
  340.0 11.7 %collective-permute-start.2 = (bf16[48,4096]{1,0:T(8,128)(2,1)}, bf16[48,4096]{1,0:T(8,128)(2,1)}, u32[]{:S(2)}, u32[]{:S(2)}) collective-permute-start(bf16[48,4096]{1,0:T(8,128)(2,1)} %get-tuple-element.80), channel_id=1, source_target_pairs={{64,0},{128,64},{192,128},{65,1},{129,65},{193,129},{66,2},{130,66... | collective-permute-start | bytes 1179656 | tf_op jit(solution)/shard_map/ppermute | solution.py:10
  352.8 10.3 %copy-start.27 = (f32[48,16]{0,1:T(8,128)S(1)}, f32[48,16]{0,1:T(8,128)}, u32[]{:S(2)}) copy-start(f32[48,16]{0,1:T(8,128)} %copy-done.26) | copy-start | bytes 9220
  363.8 3.8 copy-start.36
  363.8 5.1 copy-start.6
  367.6 13.3 %collective-permute-start.3 = (bf16[48,4096]{1,0:T(8,128)(2,1)}, bf16[48,4096]{1,0:T(8,128)(2,1)}, u32[]{:S(2)}, u32[]{:S(2)}) collective-permute-start(bf16[48,4096]{1,0:T(8,128)(2,1)} %get-tuple-element.84), channel_id=1, source_target_pairs={{64,0},{128,64},{192,128},{65,1},{129,65},{193,129},{66,2},{130,66... | collective-permute-start | bytes 1179656 | tf_op jit(solution)/shard_map/ppermute | solution.py:10
  384.7 3.7 copy-start.38
  384.8 5.2 copy-start.2
  384.8 5.2 copy-start.12
  384.8 5.2 copy-start.35
  384.8 5.4 copy-start.37
  388.5 12.1 %collective-permute-start.4 = (bf16[48,4096]{1,0:T(8,128)(2,1)S(1)}, bf16[48,4096]{1,0:T(8,128)(2,1)S(1)}, u32[]{:S(2)}, u32[]{:S(2)}) collective-permute-start(bf16[48,4096]{1,0:T(8,128)(2,1)S(1)} %get-tuple-element.88), channel_id=1, source_target_pairs={{64,0},{128,64},{192,128},{65,1},{129,65},{193,129},{66,2},{130,66... | collective-permute-start | bytes 1179656 | tf_op jit(solution)/shard_map/ppermute | solution.py:10
  402.4 10.1 %copy-start.21 = (f32[48,16]{0,1:T(8,128)S(1)}, f32[48,16]{0,1:T(8,128)}, u32[]{:S(2)}) copy-start(f32[48,16]{0,1:T(8,128)} %copy-done.20) | copy-start | bytes 9220
  413.3 4.9 copy-start.3
  413.3 5.0 copy-start.39
  416.9 10.0 %collective-permute-start.5 = (bf16[48,4096]{1,0:T(8,128)(2,1)S(1)}, bf16[48,4096]{1,0:T(8,128)(2,1)S(1)}, u32[]{:S(2)}, u32[]{:S(2)}) collective-permute-start(bf16[48,4096]{1,0:T(8,128)(2,1)S(1)} %get-tuple-element.92), channel_id=1, source_target_pairs={{64,0},{128,64},{192,128},{65,1},{129,65},{193,129},{66,2},{130,66... | collective-permute-start | bytes 1179656 | tf_op jit(solution)/shard_map/ppermute | solution.py:10
  428.8 4.1 copy-start.44
  428.8 10.1 %copy-start.48 = (f32[48]{0:T(128)S(1)}, f32[48]{0:T(128)}, u32[]{:S(2)}) copy-start(f32[48]{0:T(128)} %copy-done.47) | copy-start | bytes 580
  441.5 159.9 %all-reduce.5.cloned.1.call-start = ((), (), s32[]{:S(2)}) async-start(), calls=%async_computation.5 | async-start | bytes 524288 | tf_op jit(solution)/shard_map/psum | solution.py:94
  446.2 41.8 %copy-start.57 = (f32[48]{0:T(128)S(1)}, f32[48]{0:T(128)}, u32[]{:S(2)}) copy-start(f32[48]{0:T(128)} %get-tuple-element.55) | copy-start | bytes 580
  446.2 41.8 %copy-start.58 = (f32[48]{0:T(128)S(1)}, f32[48]{0:T(128)}, u32[]{:S(2)}) copy-start(f32[48]{0:T(128)} %get-tuple-element.56) | copy-start | bytes 580
  (28 other events, 42.2 us)
Sparse Core Ops, SparseCore 0:
  441.6 46.3 all-reduce.2
  490.4 110.9 all-reduce.4
